TPU v7x, 32 devices: a whole 2x2x4 slice. The times are simulated.
32 devices in a mesh: parts: 2 (over y), sub: 4 (over z), row: 2 (over x), col: 2 (over core).
Axes of the slice: x: 2, y: 2, z: 4, core: 2. Of those that a mesh axis runs over, the one named last changes fastest.
Arguments:
- loads: float32 [8, 32, 1024], P(('parts', 'sub'), 'col'), parts along dimension 0, may hold values from -6 to 6
- weights: float32 [8, 1024], P(('parts', 'sub')), parts along dimension 0, may hold values from 0.25 to 4
- dual_ops: bfloat16 [8, 2048, 2048], P(('parts', 'sub'), 'row'), parts along dimension 0, as said below
- corner_maps: bfloat16 [8, 24, 2048], P(('parts', 'sub'), None, 'row'), parts along dimension 0, may hold values from -0.25 to 0.25
- coarse_inverse: float32 [96, 48], P('parts'), parts along dimension 0, as said below
- corner_ids: int32 [8, 24], P('parts'), parts along dimension 0, may hold values from 0 to 47, as said below
- iface_sizes: int32 [8], P('parts'), parts along dimension 0, may hold values from 512 to 1024, as said below
- left_partner: int32 [8, 1024], P(('parts', 'sub')), parts along dimension 0, may hold values from 0 to 1023, as said below
- right_partner: int32 [8, 1024], P(('parts', 'sub')), parts along dimension 0, may hold values from 0 to 1023, as said below
Outputs:
- solution: float32 [8, 32, 1024], P(('parts', 'sub'), 'col'), parts along dimension 0
- residual: float32 [8, 32, 1024], P(('parts', 'sub'), 'col'), parts along dimension 0
There are 2 independent parts, one for each index of `parts`. A program takes and returns all parts, laid end to end along the dimension named above; each array names one. Nothing has to cross between parts.
Inputs may be any that keep to these rules, and one draw needn't show every extreme that they name: Global indices 24/2 * s to 24/2 * s + 24/2 - 1 are the corners of the interface between s and s+1; the first half of subdomain s's corner_ids is a permutation of those of interface s-1, the second half a permutation of those of interface s. `left_partner`: each row s is a permutation that maps the slots below iface_sizes[s-1] onto slots below it. `right_partner`: each row s is a permutation that maps the slots below iface_sizes[s] onto slots below it, and is the inverse of left_partner[s+1]. `dual_ops`: symmetric positive definite. `coarse_inverse`: symmetric positive definite. For each s < 2, one of iface_sizes[s] and iface_sizes[s + 2] is 896 or more and the other 640 or less.
All inputs are finite; a program needn't handle non-finite values.
Results may differ from a plain program's by a relative error of at most 0.015.
Values may be sent and summed in bfloat16 or wider, within the bound.
No kernel may reach another device: no remote copies, remote signals or barrier semaphores. Data moves between devices by JAX's collectives and lax.ppermute only.
A program may use at most 64 MiB of HBM per device.

v0:
```python
import jax
import jax.numpy as jnp
from jax import lax
from jax.sharding import PartitionSpec as P

TILE = 128
ITERS = 2


def shifted(value, axis, steps):
    count = lax.axis_size(axis)
    pairs = [(source, (source + steps) % count) for source in range(count)]
    return lax.ppermute(value, axis, pairs)


def inner(first, second, half):
    return jnp.sum(first[:, :half] * second[:, :half], axis=1)


def paired_totals(residual, precond, image, half):
    return lax.psum((inner(residual, precond, half), inner(precond, image, half)), "sub")


def tile_products(vector, rows_op, first_tile, last_tile, output):

    def one_tile(tile_at, acc):
        piece = lax.dynamic_slice_in_dim(rows_op, tile_at * TILE, TILE, 0)
        product = lax.dot_general(
            vector, piece, (((1,), (1,)), ((), ())), preferred_element_type=jnp.float32
        )
        return lax.dynamic_update_slice_in_dim(acc, product, tile_at * TILE, 1)

    return lax.fori_loop(first_tile, last_tile, one_tile, output)


def live_tiles(size_before, size_after, block_start, block, half):
    left_live = jnp.clip(size_before - block_start, 0, block)
    right_live = jnp.clip(size_after - (block_start - half), 0, block)
    live_cols = jnp.where(block_start < half, left_live, right_live)
    return (live_cols + TILE - 1) // TILE


def per_device(
    loads,
    weights,
    dual_ops,
    corner_maps,
    coarse_inverse,
    corner_ids,
    iface_sizes,
    left_partner,
    right_partner,
):
    half = loads.shape[2]
    block = dual_ops.shape[1]
    width = coarse_inverse.shape[0]
    subdomain = lax.axis_index("sub")
    count = lax.axis_size("sub")
    row_index = lax.axis_index("row")
    left_map = left_partner[0]
    right_map = right_partner[0]
    slots = jnp.arange(half, dtype=jnp.int32)
    size_before = iface_sizes[(subdomain + count - 1) % count]
    size_after = iface_sizes[subdomain]
    live_left = (slots < size_before).astype(jnp.float32)
    live_right = (right_map < size_after).astype(jnp.float32)
    columns = jnp.arange(width, dtype=jnp.int32)
    own_hot = (corner_ids[subdomain][:, None] == columns[None, :]).astype(jnp.float32)
    operator = dual_ops[0]
    coupling = corner_maps[0]
    block_start = row_index * block
    own_tiles = live_tiles(size_before, size_after, block_start, block, half)

    def apply_operator(vec):
        halfway = vec.astype(jnp.bfloat16)
        empty = jnp.zeros((halfway.shape[0], block), jnp.float32)
        local = tile_products(halfway, operator, jnp.int32(0), own_tiles, empty)
        own_slots = lax.dynamic_slice_in_dim(halfway, row_index * block, block, 1)
        corner = lax.dot_general(
            own_slots, coupling, (((1,), (1,)), ((), ())), preferred_element_type=jnp.float32
        )
        scattered = jnp.dot(corner, own_hot, precision=lax.Precision.HIGHEST)
        coarse = lax.psum(scattered, ("sub", "row"))
        solved = jnp.dot(coarse, coarse_inverse, precision=lax.Precision.HIGHEST)
        back = lax.dot_general(
            solved, own_hot, (((1,), (1,)), ((), ())), precision=lax.Precision.HIGHEST
        ).astype(jnp.bfloat16)
        united = local + jnp.dot(back, coupling, preferred_element_type=jnp.float32)
        whole = lax.all_gather(united.astype(jnp.bfloat16), "row", axis=1, tiled=True).astype(
            united.dtype
        )
        lower = whole[:, :half]
        upper = whole[:, half:]
        arrived_left = shifted(upper.astype(jnp.bfloat16), "sub", 1).astype(upper.dtype)
        arrived_right = shifted(lower.astype(jnp.bfloat16), "sub", -1).astype(lower.dtype)
        result_left = (lower + jnp.take(arrived_left, left_map, axis=1)) * live_left
        result_right = (upper + jnp.take(arrived_right, right_map, axis=1)) * live_right
        return jnp.concatenate([result_left, result_right], axis=1)

    received = (
        shifted(loads[0].astype(jnp.bfloat16), "sub", -1).astype(jnp.float32),
        shifted(weights.astype(jnp.bfloat16), "sub", -1).astype(weights.dtype),
    )
    right_load = jnp.take(received[0], right_map, axis=1) * live_right
    right_weight = jnp.take(received[1], right_map, axis=1)
    residual = jnp.concatenate([loads[0] * live_left, right_load], axis=1)
    scaling = jnp.concatenate([weights, right_weight], axis=1)
    solution = jnp.zeros_like(residual)
    precond = scaling * residual
    image = apply_operator(precond)
    gamma, delta = paired_totals(residual, precond, image, half)
    alpha = gamma / delta
    direction = precond
    along = image
    for step in range(ITERS):
        solution = solution + alpha[:, None] * direction
        residual = residual - alpha[:, None] * along
        if step + 1 < ITERS:
            precond = scaling * residual
            image = apply_operator(precond)
            gamma_next, delta = paired_totals(residual, precond, image, half)
            ratio = gamma_next / gamma
            alpha = gamma_next / (delta - ratio * gamma_next / alpha)
            direction = precond + ratio[:, None] * direction
            along = image + ratio[:, None] * along
            gamma = gamma_next
    return (solution[:, :half][None], residual[:, :half][None])


def solution(mesh):
    placed = (
        P(("parts", "sub"), "col", None),
        P(("parts", "sub"), None),
        P(("parts", "sub"), "row", None),
        P(("parts", "sub"), None, "row"),
        P("parts", None),
        P("parts", None),
        P("parts"),
        P(("parts", "sub"), None),
        P(("parts", "sub"), None),
    )
    return jax.shard_map(
        per_device,
        mesh=mesh,
        in_specs=placed,
        out_specs=(P(("parts", "sub"), "col", None), P(("parts", "sub"), "col", None)),
        check_vma=False,
    )
```

profile of v0, /device:TPU:0, one launch (start us, length us, event | category | flops | bytes accessed | tf_op | source)
XLA Modules:
  0.0 136.2 jit_solution(17909804324471528583)
XLA Ops:
  1.5 5.1 %collective-permute-start.1 = (bf16[16,1024]{1,0:T(8,128)(2,1)S(1)}, bf16[16,1024]{1,0:T(8,128)(2,1)S(1)}, u32[]{:S(2)}, u32[]{:S(2)}) collective-permute-start(bf16[16,1024]{1,0:T(8,128)(2,1)S(1)} %bitcast_convert_fusion), channel_id=1, source_target_pairs={{0,12},{4,0},{8,4},{12,8},{1,13},{5,1},{9,5},{13,9},{2,14},{6,2},{... | collective-permute-start | bytes 98312 | tf_op jit(solution)/shard_map/ppermute | solution.py:13
  9.1 1.3 fusion.49
  10.5 1.3 fusion.35
  11.8 1.3 compare_convert_fusion
  16.7 4.5 %gather_fusion = f32[1024]{0:T(1024)S(1)} fusion(f32[1024]{0:T(1024)S(1)} %bitcast.80, s32[1024]{0:T(1024)S(1)} %broadcast_clamp_fusion), kind=kCustom, calls=%fused_computation.5 | custom fusion | bytes 12288 | tf_op jit(solution)/shard_map/jit(_take)/gather | solution.py:105
  21.5 2.8 %gather_fusion.1 = f32[1024,16]{1,0:T(8,128)S(1)} fusion(f32[16,1024]{0,1:T(8,128)S(1)} %copy.21, s32[1024]{0:T(1024)S(1)} %fusion.36), kind=kCustom, calls=%fused_computation.clone | custom fusion | bytes 135168 | tf_op jit(solution)/shard_map/jit(_take)/gather | solution.py:104
  24.5 10.4 %while.20 = (s32[]{:T(128)}, f32[16,1024]{1,0:T(8,128)S(1)}, s32[]{:T(128)}, bf16[1024,2048]{1,0:T(8,128)(2,1)}, bf16[16,2048]{1,0:T(8,128)(2,1)S(1)}, /*index=5*/s32[]{:T(128)}, s32[]{:T(128)}, s32[]{:T(128)}, s32[]{:T(128)}) while((s32[]{:T(128)}, f32[16,1024]{1,0:T(8,128)S(1)}, s32[]{:T(128)}, bf16[1024,2048]{1,0:T(8,128)(2,1)}, ...), condition=%wide.region_3.5_spmd, body=%wide.region_2.4_spmd.sunk | while | flops 8388614 | bytes 599179 | solution.py:33
  25.9 1.3 fusion.72
  27.1 1.3 fusion.72
  28.4 1.3 fusion.72
  31.0 1.3 fusion.72
  32.3 1.3 fusion.72
  33.6 1.3 fusion.72
  35.3 18.9 %psum.43 = f32[16,48]{1,0:T(8,128)S(1)} all-reduce(f32[16,48]{1,0:T(8,128)S(1)} %fusion.30), channel_id=1, replica_groups=mesh['parts'=2,'sub'=4,'row'=2,'col'=2] {'sub','row'}, use_global_device_ids=true, to_apply=%region_4.6 | all-reduce | flops 768 | bytes 6144 | tf_op jit(solution)/shard_map/psum | solution.py:83
  54.6 4.6 %all_gather.6 = bf16[16,2048]{1,0:T(8,128)(2,1)S(1)} all-gather(bf16[16,1024]{1,0:T(8,128)(2,1)S(1)} %fusion.6), channel_id=1, replica_groups=mesh['parts'=2,'sub'=4,'row'=2,'col'=2] {'row'}, dimensions={1}, use_global_device_ids=true | all-gather | bytes 98304 | tf_op jit(solution)/shard_map/all_gather | solution.py:89
  59.2 3.8 %collective-permute-start.3 = (bf16[16,1024]{1,0:T(8,128)(2,1)S(1)}, bf16[16,1024]{1,0:T(8,128)(2,1)S(1)}, u32[]{:S(2)}, u32[]{:S(2)}) collective-permute-start(bf16[16,1024]{1,0:T(8,128)(2,1)S(1)} %get-tuple-element.103), channel_id=1, source_target_pairs={{0,12},{4,0},{8,4},{12,8},{1,13},{5,1},{9,5},{13,9},{2,14},{6,2},{... | collective-permute-start | bytes 98312 | tf_op jit(solution)/shard_map/ppermute | solution.py:13
  63.1 1.9 %collective-permute-done.2 = bf16[16,1024]{1,0:T(8,128)(2,1)S(1)} collective-permute-done((bf16[16,1024]{1,0:T(8,128)(2,1)S(1)}, bf16[16,1024]{1,0:T(8,128)(2,1)S(1)}, u32[]{:S(2)}, u32[]{:S(2)}) %collective-permute-start.2) | collective-permute-done | bytes 32800 | tf_op jit(solution)/shard_map/ppermute | solution.py:13
  65.1 2.8 %gather_fusion.2 = f32[1024,16]{1,0:T(8,128)S(1)} fusion(f32[16,1024]{0,1:T(8,128)S(1)} %copy.23, s32[1024]{0:T(1024)S(1)} %fusion.37), kind=kCustom, calls=%fused_computation.1.clone | custom fusion | bytes 135168 | tf_op jit(solution)/shard_map/jit(_take)/gather | solution.py:96
  68.2 2.8 %gather_fusion.3 = f32[1024,16]{1,0:T(8,128)S(1)} fusion(f32[16,1024]{0,1:T(8,128)S(1)} %copy.25, s32[1024]{0:T(1024)S(1)} %fusion.36), kind=kCustom, calls=%fused_computation.2.clone | custom fusion | bytes 135168 | tf_op jit(solution)/shard_map/jit(_take)/gather | solution.py:97
  71.3 9.1 %all-reduce.1 = (f32[16]{0:T(128)S(1)}, f32[16]{0:T(128)S(1)}) all-reduce(f32[16]{0:T(128)S(1)} %get-tuple-element.64, f32[16]{0:T(128)S(1)} %get-tuple-element.63), channel_id=1, replica_groups=mesh['parts'=2,'sub'=4,'row'=2,'col'=2] {'sub'}, use_global_device_ids=true, to_apply=%region_1.3 | all-reduce | flops 32 | bytes 256 | tf_op jit(solution)/shard_map/psum | solution.py:21
  80.6 10.3 %while.21 = (s32[]{:T(128)}, f32[16,1024]{1,0:T(8,128)S(1)}, s32[]{:T(128)}, bf16[1024,2048]{1,0:T(8,128)(2,1)}, bf16[16,2048]{1,0:T(8,128)(2,1)S(1)}, /*index=5*/s32[]{:T(128)}, s32[]{:T(128)}, s32[]{:T(128)}, s32[]{:T(128)}) while((s32[]{:T(128)}, f32[16,1024]{1,0:T(8,128)S(1)}, s32[]{:T(128)}, bf16[1024,2048]{1,0:T(8,128)(2,1)}, ...), condition=%wide.region_10.12_spmd, body=%wide.region_9.11_spmd.sunk | while | flops 8388614 | bytes 599179 | solution.py:33
  81.9 1.3 fusion.75
  84.5 1.3 fusion.75
  85.8 1.3 fusion.75
  87.1 1.3 fusion.75
  91.2 18.7 %psum.46 = f32[16,48]{1,0:T(8,128)S(1)} all-reduce(f32[16,48]{1,0:T(8,128)S(1)} %fusion.29), channel_id=1, replica_groups=mesh['parts'=2,'sub'=4,'row'=2,'col'=2] {'sub','row'}, use_global_device_ids=true, to_apply=%region_11.13 | all-reduce | flops 768 | bytes 6144 | tf_op jit(solution)/shard_map/psum | solution.py:83
  110.3 4.6 %all_gather.7 = bf16[16,2048]{1,0:T(8,128)(2,1)S(1)} all-gather(bf16[16,1024]{1,0:T(8,128)(2,1)S(1)} %fusion.7), channel_id=1, replica_groups=mesh['parts'=2,'sub'=4,'row'=2,'col'=2] {'row'}, dimensions={1}, use_global_device_ids=true | all-gather | bytes 98304 | tf_op jit(solution)/shard_map/all_gather | solution.py:89
  114.9 2.0 %collective-permute-start.4 = (bf16[16,1024]{1,0:T(8,128)(2,1)S(1)}, bf16[16,1024]{1,0:T(8,128)(2,1)S(1)}, u32[]{:S(2)}, u32[]{:S(2)}) collective-permute-start(bf16[16,1024]{1,0:T(8,128)(2,1)S(1)} %get-tuple-element.101), channel_id=1, source_target_pairs={{0,4},{4,8},{8,12},{12,0},{1,5},{5,9},{9,13},{13,1},{2,6},{6,10},{... | collective-permute-start | bytes 98312 | tf_op jit(solution)/shard_map/ppermute | solution.py:13
  117.0 1.9 %collective-permute-done.5 = bf16[16,1024]{1,0:T(8,128)(2,1)S(1)} collective-permute-done((bf16[16,1024]{1,0:T(8,128)(2,1)S(1)}, bf16[16,1024]{1,0:T(8,128)(2,1)S(1)}, u32[]{:S(2)}, u32[]{:S(2)}) %collective-permute-start.5) | collective-permute-done | bytes 32800 | tf_op jit(solution)/shard_map/ppermute | solution.py:13
  119.0 2.8 %gather_fusion.5 = f32[1024,16]{1,0:T(8,128)S(1)} fusion(f32[16,1024]{0,1:T(8,128)S(1)} %copy.29, s32[1024]{0:T(1024)S(1)} %fusion.36), kind=kCustom, calls=%fused_computation.4.clone | custom fusion | bytes 135168 | tf_op jit(solution)/shard_map/jit(_take)/gather | solution.py:97
  122.1 2.8 %gather_fusion.4 = f32[1024,16]{1,0:T(8,128)S(1)} fusion(f32[16,1024]{0,1:T(8,128)S(1)} %copy.27, s32[1024]{0:T(1024)S(1)} %fusion.37), kind=kCustom, calls=%fused_computation.3.clone | custom fusion | bytes 135168 | tf_op jit(solution)/shard_map/jit(_take)/gather | solution.py:96
  125.3 10.2 %all-reduce = (f32[16]{0:T(128)S(1)}, f32[16]{0:T(128)S(1)}) all-reduce(f32[16]{0:T(128)S(1)} %get-tuple-element.62, f32[16]{0:T(128)S(1)} %get-tuple-element.61), channel_id=1, replica_groups=mesh['parts'=2,'sub'=4,'row'=2,'col'=2] {'sub'}, use_global_device_ids=true, to_apply=%region_8.10 | all-reduce | flops 32 | bytes 256 | tf_op jit(solution)/shard_map/psum | solution.py:21
  (71 shorter events, 17.8 us)
Async XLA Ops:
  0.6 34.3 %copy-start = (bf16[1,24,1024]{2,1,0:T(8,128)(2,1)S(1)}, bf16[1,24,1024]{2,1,0:T(8,128)(2,1)}, u32[]{:S(2)}) copy-start(bf16[1,24,1024]{2,1,0:T(8,128)(2,1)} %param.18) | copy-start | bytes 147460
  0.6 20.7 %copy-start.5 = (f32[1,1024]{1,0:T(1,128)S(1)}, f32[1,1024]{1,0:T(1,128)}, u32[]{:S(2)}) copy-start(f32[1,1024]{1,0:T(1,128)} %param.16) | copy-start | bytes 12292
  0.7 20.6 %copy-start.2 = (s32[1,1024]{1,0:T(1,128)S(1)}, s32[1,1024]{1,0:T(1,128)}, u32[]{:S(2)}) copy-start(s32[1,1024]{1,0:T(1,128)} %param.23) | copy-start | bytes 12292
  1.5 19.8 %collective-permute-start.1 = (bf16[16,1024]{1,0:T(8,128)(2,1)S(1)}, bf16[16,1024]{1,0:T(8,128)(2,1)S(1)}, u32[]{:S(2)}, u32[]{:S(2)}) collective-permute-start(bf16[16,1024]{1,0:T(8,128)(2,1)S(1)} %bitcast_convert_fusion), channel_id=1, source_target_pairs={{0,12},{4,0},{8,4},{12,8},{1,13},{5,1},{9,5},{13,9},{2,14},{6,2},{... | collective-permute-start | bytes 98312 | tf_op jit(solution)/shard_map/ppermute | solution.py:13
  7.3 9.4 %collective-permute-start = (bf16[1,1024]{1,0:T(2,128)(2,1)S(1)}, bf16[1,1024]{1,0:T(2,128)(2,1)S(1)}, u32[]{:S(2)}, u32[]{:S(2)}) collective-permute-start(bf16[1,1024]{1,0:T(2,128)(2,1)S(1)} %convert_element_type.71), channel_id=1, source_target_pairs={{0,12},{4,0},{8,4},{12,8},{1,13},{5,1},{9,5},{13,9},{2,14},{6,2},{... | collective-permute-start | bytes 6152 | tf_op jit(solution)/shard_map/ppermute | solution.py:13
  16.7 37.4 %copy-start.3 = (f32[48,48]{1,0:T(8,128)S(1)}, f32[48,48]{1,0:T(8,128)}, u32[]{:S(2)}) copy-start(f32[48,48]{1,0:T(8,128)} %param.19) | copy-start | bytes 27652
  16.7 46.3 %copy-start.4 = (s32[1,1024]{1,0:T(1,128)S(1)}, s32[1,1024]{1,0:T(1,128)}, u32[]{:S(2)}) copy-start(s32[1,1024]{1,0:T(1,128)} %param.22) | copy-start | bytes 12292
  24.5 46.7 %copy-start.1 = (f32[1,16,1024]{2,1,0:T(8,128)S(1)}, f32[1,16,1024]{2,1,0:T(8,128)}, u32[]{:S(2)}) copy-start(f32[1,16,1024]{2,1,0:T(8,128)} %param.15) | copy-start | bytes 196612
  59.2 5.7 %collective-permute-start.2 = (bf16[16,1024]{1,0:T(8,128)(2,1)S(1)}, bf16[16,1024]{1,0:T(8,128)(2,1)S(1)}, u32[]{:S(2)}, u32[]{:S(2)}) collective-permute-start(bf16[16,1024]{1,0:T(8,128)(2,1)S(1)} %get-tuple-element.102), channel_id=1, source_target_pairs={{0,4},{4,8},{8,12},{12,0},{1,5},{5,9},{9,13},{13,1},{2,6},{6,10},{... | collective-permute-start | bytes 98312 | tf_op jit(solution)/shard_map/ppermute | solution.py:13
  59.2 8.8 %collective-permute-start.3 = (bf16[16,1024]{1,0:T(8,128)(2,1)S(1)}, bf16[16,1024]{1,0:T(8,128)(2,1)S(1)}, u32[]{:S(2)}, u32[]{:S(2)}) collective-permute-start(bf16[16,1024]{1,0:T(8,128)(2,1)S(1)} %get-tuple-element.103), channel_id=1, source_target_pairs={{0,12},{4,0},{8,4},{12,8},{1,13},{5,1},{9,5},{13,9},{2,14},{6,2},{... | collective-permute-start | bytes 98312 | tf_op jit(solution)/shard_map/ppermute | solution.py:13
  114.9 3.9 %collective-permute-start.5 = (bf16[16,1024]{1,0:T(8,128)(2,1)S(1)}, bf16[16,1024]{1,0:T(8,128)(2,1)S(1)}, u32[]{:S(2)}, u32[]{:S(2)}) collective-permute-start(bf16[16,1024]{1,0:T(8,128)(2,1)S(1)} %get-tuple-element.100), channel_id=1, source_target_pairs={{0,12},{4,0},{8,4},{12,8},{1,13},{5,1},{9,5},{13,9},{2,14},{6,2},{... | collective-permute-start | bytes 98312 | tf_op jit(solution)/shard_map/ppermute | solution.py:13
  114.9 7.0 %collective-permute-start.4 = (bf16[16,1024]{1,0:T(8,128)(2,1)S(1)}, bf16[16,1024]{1,0:T(8,128)(2,1)S(1)}, u32[]{:S(2)}, u32[]{:S(2)}) collective-permute-start(bf16[16,1024]{1,0:T(8,128)(2,1)S(1)} %get-tuple-element.101), channel_id=1, source_target_pairs={{0,4},{4,8},{8,12},{12,0},{1,5},{5,9},{9,13},{13,1},{2,6},{6,10},{... | collective-permute-start | bytes 98312 | tf_op jit(solution)/shard_map/ppermute | solution.py:13
where the time goes:
time: 137 us; the launch traced here: 136 us
  blocking collectives  65.9 us (48%)
  matrix products  22.3 us (16%)
  local copies, waits for them, and re-layouts  22.1 us (16%)
  starting transfers between devices  11.4 us (8%)
  other arithmetic  8.41 us (6%)
  waiting for transfers between devices  3.74 us (3%)
  between operations  2.25 us (2%)
    psum x2, blocking collectives, apply_operator(): coarse = lax.psum(scattered, ('sub', 'row'))  37.5 us
    dot_general x16, matrix products, one_tile(): lax.dot_general(vector, piece, (((1,), (1,)), ((), ())), preferred_elemen...  20.7 us
    psum x2, blocking collectives, paired_totals(): lax.psum((inner(residual, precond, half), inner(precond, image, half)), '...  19.2 us
    ppermute x6, starting transfers between devices, shifted(): return lax.ppermute(value, axis, pairs)  11.4 us
    all_gather x2, blocking collectives, apply_operator(): lax.all_gather(united.astype(jnp.bfloat16), 'row', axis=1, tiled=True)  9.15 us
    gather x4, local copies, waits for them, and re-layouts, apply_operator(): jnp.take(arrived_right, right_map, axis=1)  5.95 us
    gather x4, local copies, waits for them, and re-layouts, apply_operator(): result_left = (lower + jnp.take(arrived_left, left_map, axis=1)) * live_left  5.95 us
    gather x1, local copies, waits for them, and re-layouts, per_device(): right_weight = jnp.take(received[1], right_map, axis=1)  4.53 us
  transfers between devices with their start and end apart: 6, of which 2 were waited for; matrix products, arithmetic and copies ran while one was open for 14% of the time, Pallas kernels for 0%

commit v1 on v0

--- a/solution.py
+++ b/solution.py
@@ -5,6 +5,12 @@
 
 TILE = 128
 ITERS = 2
+
+
+def _assign_spot(x_part, mesh_dim):
+    extra = lax.all_gather(x_part, mesh_dim)
+    last = jnp.concatenate(extra, axis=1)
+    return last
 
 
 def shifted(value, axis, steps):
@@ -86,9 +92,7 @@
             solved, own_hot, (((1,), (1,)), ((), ())), precision=lax.Precision.HIGHEST
         ).astype(jnp.bfloat16)
         united = local + jnp.dot(back, coupling, preferred_element_type=jnp.float32)
-        whole = lax.all_gather(united.astype(jnp.bfloat16), "row", axis=1, tiled=True).astype(
-            united.dtype
-        )
+        whole = _assign_spot(united.astype(jnp.bfloat16), "row").astype(united.dtype)
         lower = whole[:, :half]
         upper = whole[:, half:]
         arrived_left = shifted(upper.astype(jnp.bfloat16), "sub", 1).astype(upper.dtype)

time: 137 us -> 174 us (1.27)
  local copies, waits for them, and re-layouts: 22.1 us -> 36.8 us
  other arithmetic: 8.41 us -> 21.7 us
  waiting for transfers between devices: 3.74 us -> 12.6 us
    ppermute x6, waiting for transfers between devices: 3.74 us -> 12.6 us  [shifted(): return lax.ppermute(value, axis, pairs)]
    reduce_sum x2, other arithmetic: 0.29 us -> 5.71 us  [inner(): return jnp.sum(first[:, :half] * second[:, :half], axis=1)]
    unnamed x12 -> x16, local copies, waits for them, and re-layouts: 0.04 us -> 3.9 us
    convert_element_type x2, other arithmetic: 0.12 us -> 3.83 us  [apply_operator(): halfway = vec.astype(jnp.bfloat16)]
    convert_element_type x2 -> x7, other arithmetic: 0.02 us -> 3.7 us  [the longest x2 1.82 us: apply_operator(): shifted(upper.astype(jnp.bfloat16), 'sub', 1).astype(upper.dtype)]
    gather x4 -> x2, local copies, waits for them, and re-layouts: 5.95 us -> 9.09 us  [apply_operator(): result_left = (lower + jnp.take(arrived_left, left_map, axis=1)) * live_left]
    gather x4 -> x2, local copies, waits for them, and re-layouts: 5.95 us -> 9.08 us  [apply_operator(): jnp.take(arrived_right, right_map, axis=1)]
    mul x0 -> x3, local copies, waits for them, and re-layouts: none -> 2.73 us  [the longest x1 1.36 us: per_device(): residual = residual - alpha[:, None] * along]
where the time goes in v1:
time: 174 us; the launch traced here: 173 us
  blocking collectives  65.4 us (38%)
  local copies, waits for them, and re-layouts  36.8 us (21%)
  matrix products  22.5 us (13%)
  other arithmetic  21.7 us (12%)
  waiting for transfers between devices  12.6 us (7%)
  starting transfers between devices  11.4 us (7%)
  between operations  2.25 us (1%)
    psum x2, blocking collectives, apply_operator(): coarse = lax.psum(scattered, ('sub', 'row'))  36.8 us
    dot_general x16, matrix products, one_tile(): lax.dot_general(vector, piece, (((1,), (1,)), ((), ())), preferred_elemen...  20.7 us
    psum x2, blocking collectives, paired_totals(): lax.psum((inner(residual, precond, half), inner(precond, image, half)), '...  19.5 us
    ppermute x6, waiting for transfers between devices, shifted(): return lax.ppermute(value, axis, pairs)  12.6 us
    ppermute x6, starting transfers between devices, shifted(): return lax.ppermute(value, axis, pairs)  11.4 us
    all_gather x2, blocking collectives, _assign_spot(): extra = lax.all_gather(x_part, mesh_dim)  9.15 us
    gather x2, local copies, waits for them, and re-layouts, apply_operator(): result_left = (lower + jnp.take(arrived_left, left_map, axis=1)) * live_left  9.09 us
    gather x2, local copies, waits for them, and re-layouts, apply_operator(): jnp.take(arrived_right, right_map, axis=1)  9.08 us
  transfers between devices with their start and end apart: 6, of which 2 were waited for; matrix products, arithmetic and copies ran while one was open for 14% of the time, Pallas kernels for 0%

profile of v1, /device:TPU:0, one launch (start us, length us, event | category | flops | bytes accessed | tf_op | source)
XLA Modules:
  0.0 172.7 jit_solution(17816688243890508609)
XLA Ops:
  1.4 5.1 %collective-permute-start = (bf16[1,1024]{1,0:T(2,128)(2,1)S(1)}, bf16[1,1024]{1,0:T(2,128)(2,1)S(1)}, u32[]{:S(2)}, u32[]{:S(2)}) collective-permute-start(bf16[1,1024]{1,0:T(2,128)(2,1)S(1)} %convert_element_type.83), channel_id=1, source_target_pairs={{0,12},{4,0},{8,4},{12,8},{1,13},{5,1},{9,5},{13,9},{2,14},{6,2},{... | collective-permute-start | bytes 6152 | tf_op jit(solution)/shard_map/ppermute | solution.py:19
  9.4 1.3 fusion.48
  10.8 1.3 compare_convert_fusion
  13.5 1.3 fusion.34
  16.4 4.5 %gather_fusion = f32[1024]{0:T(1024)S(1)} fusion(f32[1024]{0:T(1024)S(1)} %bitcast.90, s32[1024]{0:T(1024)S(1)} %broadcast_clamp_fusion), kind=kCustom, calls=%fused_computation.5 | custom fusion | bytes 12288 | tf_op jit(solution)/shard_map/jit(_take)/gather | solution.py:109
  21.0 2.8 %gather_fusion.1 = f32[1024,16]{1,0:T(8,128)S(1)} fusion(f32[16,1024]{0,1:T(8,128)S(1)} %convert_element_type.86, s32[1024]{0:T(1024)S(1)} %fusion.35), kind=kCustom, calls=%fused_computation.clone | custom fusion | bytes 135168 | tf_op jit(solution)/shard_map/jit(_take)/gather | solution.py:108
  24.2 1.3 fusion.44
  26.1 18.9 %psum.43 = f32[16,48]{1,0:T(8,128)S(1)} all-reduce(f32[16,48]{1,0:T(8,128)S(1)} %fusion.29), channel_id=1, replica_groups=mesh['parts'=2,'sub'=4,'row'=2,'col'=2] {'sub','row'}, use_global_device_ids=true, to_apply=%region_4.6 | all-reduce | flops 768 | bytes 6144 | tf_op jit(solution)/shard_map/psum | solution.py:89
  45.4 10.4 %while.20 = (s32[]{:T(128)}, f32[16,1024]{1,0:T(8,128)S(1)}, s32[]{:T(128)}, bf16[1024,2048]{1,0:T(8,128)(2,1)}, bf16[16,2048]{1,0:T(8,128)(2,1)S(1)}, /*index=5*/s32[]{:T(128)}, s32[]{:T(128)}, s32[]{:T(128)}, s32[]{:T(128)}) while((s32[]{:T(128)}, f32[16,1024]{1,0:T(8,128)S(1)}, s32[]{:T(128)}, bf16[1024,2048]{1,0:T(8,128)(2,1)}, ...), condition=%wide.region_3.5_spmd, body=%wide.region_2.4_spmd.sunk | while | flops 8388614 | bytes 599179 | solution.py:39
  46.7 1.3 fusion.71
  48.0 1.3 fusion.71
  55.9 4.6 %all-gather = bf16[32,1024]{1,0:T(8,128)(2,1)S(1)} all-gather(bf16[16,1024]{1,0:T(8,128)(2,1)S(1)} %fusion.6), channel_id=2, replica_groups=mesh['parts'=2,'sub'=4,'row'=2,'col'=2] {'row'}, dimensions={0}, use_global_device_ids=true | all-gather | bytes 98304 | tf_op jit(solution)/shard_map/all_gather | solution.py:11
  61.6 3.8 %collective-permute-start.3 = (bf16[16,1024]{0,1:T(8,128)(2,1)S(1)}, bf16[16,1024]{0,1:T(8,128)(2,1)}, u32[]{:S(2)}, u32[]{:S(2)}) collective-permute-start(bf16[16,1024]{0,1:T(8,128)(2,1)S(1)} %get-tuple-element.151), channel_id=1, source_target_pairs={{0,12},{4,0},{8,4},{12,8},{1,13},{5,1},{9,5},{13,9},{2,14},{6,2},{... | collective-permute-start | bytes 98312 | tf_op jit(solution)/shard_map/ppermute | solution.py:19
  65.4 5.5 %collective-permute-done.3 = bf16[16,1024]{0,1:T(8,128)(2,1)} collective-permute-done((bf16[16,1024]{0,1:T(8,128)(2,1)S(1)}, bf16[16,1024]{0,1:T(8,128)(2,1)}, u32[]{:S(2)}, u32[]{:S(2)}) %collective-permute-start.3) | collective-permute-done | bytes 32800 | tf_op jit(solution)/shard_map/ppermute | solution.py:19
  71.9 4.0 %gather_fusion.3 = f32[1024,16]{1,0:T(8,128)} fusion(f32[16,1024]{0,1:T(8,128)S(1)} %convert_element_type.96, s32[1024]{0:T(1024)S(1)} %fusion.35), kind=kCustom, calls=%fused_computation.2.clone | custom fusion | bytes 135168 | tf_op jit(solution)/shard_map/jit(_take)/gather | solution.py:101
  76.0 4.0 %gather_fusion.2 = f32[1024,16]{1,0:T(8,128)} fusion(f32[16,1024]{0,1:T(8,128)S(1)} %convert_element_type.94, s32[1024]{0:T(1024)S(1)} %fusion.36), kind=kCustom, calls=%fused_computation.1.clone | custom fusion | bytes 135168 | tf_op jit(solution)/shard_map/jit(_take)/gather | solution.py:100
  80.0 2.8 %multiply_reduce_fusion.2 = (f32[16]{0:T(128)S(1)}, f32[16]{0:T(128)S(1)}, f32[16,1024]{0,1:T(8,128)}, f32[16,1024]{0,1:T(8,128)S(1)}) fusion(f32[16,2048]{0,1:T(8,128)} %get-tuple-element.145, f32[1024]{0:T(1024)S(1)} %get-tuple-element.156, f32[1024,16]{1,0:T(8,128)} %gather_fusion.2, pred[1024]{0:T(1024)(128)(4,1)S(1)} %compare_and_fusion, ...), kind=kLoop, calls=%fused_computation.42 | loop fusion | flops 180192 | bytes 534656 | tf_op jit(solution)/shard_map/reduce_sum | solution.py:23
  84.2 11.2 %all-reduce.1 = (f32[16]{0:T(128)S(1)}, f32[16]{0:T(128)S(1)}) all-reduce(f32[16]{0:T(128)S(1)} %get-tuple-element.112, f32[16]{0:T(128)S(1)} %get-tuple-element.111), channel_id=1, replica_groups=mesh['parts'=2,'sub'=4,'row'=2,'col'=2] {'sub'}, use_global_device_ids=true, to_apply=%region_1.3 | all-reduce | flops 32 | bytes 256 | tf_op jit(solution)/shard_map/psum | solution.py:27
  95.4 1.4 copy.51
  96.8 2.5 %fusion.41 = (bf16[16,2048]{0,1:T(8,128)(2,1)S(1)}, f32[16,2048]{0,1:T(8,128)S(1)}, f32[16,2048]{0,1:T(8,128)}) fusion(f32[2048]{0:T(1024)S(1)} %bitcast.101, f32[16,2048]{0,1:T(8,128)} %copy.51, f32[16,1024]{0,1:T(8,128)S(1)} %bitcast_multiply_fusion, f32[16,1024]{0,1:T(8,128)S(1)} %bitcast_multiply_fusion.1), kind=kLoop, calls=%fused_computation.88 | loop fusion | flops 131072 | bytes 598016 | tf_op jit(solution)/shard_map/convert_element_type | solution.py:81
  99.9 17.9 %psum.46 = f32[16,48]{1,0:T(8,128)S(1)} all-reduce(f32[16,48]{1,0:T(8,128)S(1)} %fusion.28), channel_id=1, replica_groups=mesh['parts'=2,'sub'=4,'row'=2,'col'=2] {'sub','row'}, use_global_device_ids=true, to_apply=%region_11.13 | all-reduce | flops 768 | bytes 6144 | tf_op jit(solution)/shard_map/psum | solution.py:89
  118.2 10.4 %while.21 = (s32[]{:T(128)}, f32[16,1024]{1,0:T(8,128)S(1)}, s32[]{:T(128)}, bf16[1024,2048]{1,0:T(8,128)(2,1)}, bf16[16,2048]{1,0:T(8,128)(2,1)S(1)}, /*index=5*/s32[]{:T(128)}, s32[]{:T(128)}, s32[]{:T(128)}, s32[]{:T(128)}) while((s32[]{:T(128)}, f32[16,1024]{1,0:T(8,128)S(1)}, s32[]{:T(128)}, bf16[1024,2048]{1,0:T(8,128)(2,1)}, ...), condition=%wide.region_10.12_spmd, body=%wide.region_9.11_spmd.sunk | while | flops 8388614 | bytes 599179 | solution.py:39
  128.7 4.6 %all-gather.1 = bf16[32,1024]{1,0:T(8,128)(2,1)S(1)} all-gather(bf16[16,1024]{1,0:T(8,128)(2,1)S(1)} %fusion.7), channel_id=3, replica_groups=mesh['parts'=2,'sub'=4,'row'=2,'col'=2] {'row'}, dimensions={0}, use_global_device_ids=true | all-gather | bytes 98304 | tf_op jit(solution)/shard_map/all_gather | solution.py:11
  134.4 2.0 %collective-permute-start.4 = (bf16[16,1024]{0,1:T(8,128)(2,1)}, bf16[16,1024]{0,1:T(8,128)(2,1)}, u32[]{:S(2)}, u32[]{:S(2)}) collective-permute-start(bf16[16,1024]{0,1:T(8,128)(2,1)} %get-tuple-element.148), channel_id=1, source_target_pairs={{0,4},{4,8},{8,12},{12,0},{1,5},{5,9},{9,13},{13,1},{2,6},{6,10},{... | collective-permute-start | bytes 98312 | tf_op jit(solution)/shard_map/ppermute | solution.py:19
  136.4 7.2 %collective-permute-done.5 = bf16[16,1024]{0,1:T(8,128)(2,1)S(1)} collective-permute-done((bf16[16,1024]{0,1:T(8,128)(2,1)S(1)}, bf16[16,1024]{0,1:T(8,128)(2,1)S(1)}, u32[]{:S(2)}, u32[]{:S(2)}) %collective-permute-start.5) | collective-permute-done | bytes 32800 | tf_op jit(solution)/shard_map/ppermute | solution.py:19
  144.4 5.1 %gather_fusion.5 = f32[1024,16]{1,0:T(8,128)} fusion(f32[16,1024]{0,1:T(8,128)} %convert_element_type.106, s32[1024]{0:T(1024)S(1)} %fusion.35), kind=kCustom, calls=%fused_computation.4.clone | custom fusion | bytes 135168 | tf_op jit(solution)/shard_map/jit(_take)/gather | solution.py:101
  149.5 1.8 %convert_element_type.104 = f32[16,1024]{0,1:T(8,128)} convert(bf16[16,1024]{0,1:T(8,128)(2,1)} %collective-permute-done.4) | non-fusion elementwise | flops 16384 | bytes 98304 | tf_op jit(solution)/shard_map/convert_element_type | solution.py:98
  151.3 5.1 %gather_fusion.4 = f32[1024,16]{1,0:T(8,128)} fusion(f32[16,1024]{0,1:T(8,128)} %convert_element_type.104, s32[1024]{0:T(1024)S(1)} %fusion.36), kind=kCustom, calls=%fused_computation.3.clone | custom fusion | bytes 135168 | tf_op jit(solution)/shard_map/jit(_take)/gather | solution.py:100
  156.3 2.9 %multiply_reduce_fusion = (f32[16]{0:T(128)S(1)}, f32[16]{0:T(128)S(1)}, f32[16,1024]{0,1:T(8,128)}, f32[16,1024]{0,1:T(8,128)}) fusion(f32[16,2048]{0,1:T(8,128)S(1)} %get-tuple-element.141, f32[16,2048]{0,1:T(8,128)} %get-tuple-element.142, f32[1024]{0:T(1024)S(1)} %get-tuple-element.156, f32[1024,16]{1,0:T(8,128)} %gather_fusion.4, ...), kind=kLoop, calls=%fused_computation.40 | loop fusion | flops 163808 | bytes 534656 | tf_op jit(solution)/shard_map/reduce_sum | solution.py:23
  159.2 8.3 %all-reduce = (f32[16]{0:T(128)S(1)}, f32[16]{0:T(128)S(1)}) all-reduce(f32[16]{0:T(128)S(1)} %get-tuple-element.110, f32[16]{0:T(128)S(1)} %get-tuple-element.109), channel_id=1, replica_groups=mesh['parts'=2,'sub'=4,'row'=2,'col'=2] {'sub'}, use_global_device_ids=true, to_apply=%region_8.10 | all-reduce | flops 32 | bytes 256 | tf_op jit(solution)/shard_map/psum | solution.py:27
  167.9 2.2 %fusion.13 = (f32[1,16,1024]{1,2,0:T(8,128)}, f32[1,16,1024]{1,2,0:T(8,128)S(1)}) fusion(f32[16,1024]{0,1:T(8,128)S(1)} %copy.59, f32[16,1024]{0,1:T(8,128)} %get-tuple-element.146, f32[16,1024]{0,1:T(8,128)} %get-tuple-element.139, f32[16,2048]{0,1:T(8,128)} %get-tuple-element.142, f32[16]{0:T(128)S(1)} %get-tuple-element.137, ...), kind=kLoop, calls=%fused_computation.27 | loop fusion | flops 147456 | bytes 524480 | tf_op jit(solution)/shard_map/broadcast_in_dim | solution.py:131
  170.1 1.8 %copy.57 = f32[1,16,1024]{2,1,0:T(8,128)} copy(f32[1,16,1024]{1,2,0:T(8,128)} %get-tuple-element.152) | data formatting | bytes 131072
  (80 shorter events, 32.7 us)
Async XLA Ops:
  0.6 25.1 %copy-start = (bf16[1,24,1024]{2,1,0:T(8,128)(2,1)S(1)}, bf16[1,24,1024]{2,1,0:T(8,128)(2,1)}, u32[]{:S(2)}) copy-start(bf16[1,24,1024]{2,1,0:T(8,128)(2,1)} %param.18) | copy-start | bytes 147460
  0.6 20.3 %copy-start.5 = (f32[1,1024]{1,0:T(1,128)S(1)}, f32[1,1024]{1,0:T(1,128)}, u32[]{:S(2)}) copy-start(f32[1,1024]{1,0:T(1,128)} %param.16) | copy-start | bytes 12292
  0.7 20.3 %copy-start.2 = (s32[1,1024]{1,0:T(1,128)S(1)}, s32[1,1024]{1,0:T(1,128)}, u32[]{:S(2)}) copy-start(s32[1,1024]{1,0:T(1,128)} %param.23) | copy-start | bytes 12292
  1.4 15.0 %collective-permute-start = (bf16[1,1024]{1,0:T(2,128)(2,1)S(1)}, bf16[1,1024]{1,0:T(2,128)(2,1)S(1)}, u32[]{:S(2)}, u32[]{:S(2)}) collective-permute-start(bf16[1,1024]{1,0:T(2,128)(2,1)S(1)} %convert_element_type.83), channel_id=1, source_target_pairs={{0,12},{4,0},{8,4},{12,8},{1,13},{5,1},{9,5},{13,9},{2,14},{6,2},{... | collective-permute-start | bytes 6152 | tf_op jit(solution)/shard_map/ppermute | solution.py:19
  7.6 13.4 %collective-permute-start.1 = (bf16[16,1024]{0,1:T(8,128)(2,1)S(1)}, bf16[16,1024]{0,1:T(8,128)(2,1)S(1)}, u32[]{:S(2)}, u32[]{:S(2)}) collective-permute-start(bf16[16,1024]{0,1:T(8,128)(2,1)S(1)} %bitcast_convert_fusion), channel_id=1, source_target_pairs={{0,12},{4,0},{8,4},{12,8},{1,13},{5,1},{9,5},{13,9},{2,14},{6,2},{... | collective-permute-start | bytes 98312 | tf_op jit(solution)/shard_map/ppermute | solution.py:19
  16.4 28.6 %copy-start.3 = (f32[48,48]{1,0:T(8,128)S(1)}, f32[48,48]{1,0:T(8,128)}, u32[]{:S(2)}) copy-start(f32[48,48]{1,0:T(8,128)} %param.19) | copy-start | bytes 27652
  24.2 41.2 %copy-start.4 = (s32[1,1024]{1,0:T(1,128)S(1)}, s32[1,1024]{1,0:T(1,128)}, u32[]{:S(2)}) copy-start(s32[1,1024]{1,0:T(1,128)} %param.22) | copy-start | bytes 12292
  61.6 14.3 %collective-permute-start.2 = (bf16[16,1024]{0,1:T(8,128)(2,1)}, bf16[16,1024]{0,1:T(8,128)(2,1)S(1)}, u32[]{:S(2)}, u32[]{:S(2)}) collective-permute-start(bf16[16,1024]{0,1:T(8,128)(2,1)} %get-tuple-element.150), channel_id=1, source_target_pairs={{0,4},{4,8},{8,12},{12,0},{1,5},{5,9},{9,13},{13,1},{2,6},{6,10},{... | collective-permute-start | bytes 98312 | tf_op jit(solution)/shard_map/ppermute | solution.py:19
  61.6 9.3 %collective-permute-start.3 = (bf16[16,1024]{0,1:T(8,128)(2,1)S(1)}, bf16[16,1024]{0,1:T(8,128)(2,1)}, u32[]{:S(2)}, u32[]{:S(2)}) collective-permute-start(bf16[16,1024]{0,1:T(8,128)(2,1)S(1)} %get-tuple-element.151), channel_id=1, source_target_pairs={{0,12},{4,0},{8,4},{12,8},{1,13},{5,1},{9,5},{13,9},{2,14},{6,2},{... | collective-permute-start | bytes 98312 | tf_op jit(solution)/shard_map/ppermute | solution.py:19
  134.4 33.5 %copy-start.1 = (f32[16,2048]{0,1:T(8,128)S(1)}, f32[16,2048]{0,1:T(8,128)}, u32[]{:S(2)}) copy-start(f32[16,2048]{0,1:T(8,128)} %get-tuple-element.145) | copy-start | bytes 393220
  134.4 9.2 %collective-permute-start.5 = (bf16[16,1024]{0,1:T(8,128)(2,1)S(1)}, bf16[16,1024]{0,1:T(8,128)(2,1)S(1)}, u32[]{:S(2)}, u32[]{:S(2)}) collective-permute-start(bf16[16,1024]{0,1:T(8,128)(2,1)S(1)} %get-tuple-element.147), channel_id=1, source_target_pairs={{0,12},{4,0},{8,4},{12,8},{1,13},{5,1},{9,5},{13,9},{2,14},{6,2},{... | collective-permute-start | bytes 98312 | tf_op jit(solution)/shard_map/ppermute | solution.py:19
  134.4 15.1 %collective-permute-start.4 = (bf16[16,1024]{0,1:T(8,128)(2,1)}, bf16[16,1024]{0,1:T(8,128)(2,1)}, u32[]{:S(2)}, u32[]{:S(2)}) collective-permute-start(bf16[16,1024]{0,1:T(8,128)(2,1)} %get-tuple-element.148), channel_id=1, source_target_pairs={{0,4},{4,8},{8,12},{12,0},{1,5},{5,9},{9,13},{13,1},{2,6},{6,10},{... | collective-permute-start | bytes 98312 | tf_op jit(solution)/shard_map/ppermute | solution.py:19
